TPU v7x, 128 devices: a whole 4x4x4 slice. The times are simulated.
128 devices in a mesh: req: 32 (over x, z, core), tp: 4 (over y).
Axes of the slice: x: 4, y: 4, z: 4, core: 2. Of those that a mesh axis runs over, the one named last changes fastest.
Arguments:
- tokens: bfloat16 [65536, 1024], P('req'), may hold values from -6 to 6
- attn_gain: bfloat16 [1024], replicated, may hold values from 0.5 to 1.5
- w_query: bfloat16 [1024, 1024], P(None, 'tp'), may hold values from -1 to 1
- w_key: bfloat16 [1024, 1024], P(None, 'tp'), may hold values from -1 to 1
- w_value: bfloat16 [1024, 1024], P(None, 'tp'), may hold values from -0.1875 to 0.1875
- persist_key: bfloat16 [16, 1024], P(None, 'tp'), may hold values from -250 to 250
- persist_value: bfloat16 [16, 1024], P(None, 'tp'), may hold values from -6 to 6
- log_forget: float32 [65536, 8], P('req', 'tp'), may hold values from -0.75 to 0
- mem_gain: float32 [1024], P('tp'), may hold values from 0.5 to 1.5
- w_out: bfloat16 [1024, 1024], P('tp'), may hold values from -0.1875 to 0.1875
- ffn_gain: bfloat16 [1024], replicated, may hold values from 0.5 to 1.5
- w_gate: bfloat16 [1024, 2816], P(None, 'tp'), may hold values from -0.1875 to 0.1875
- w_up: bfloat16 [1024, 2816], P(None, 'tp'), may hold values from -0.1875 to 0.1875
- w_down: bfloat16 [2816, 1024], P('tp'), may hold values from -0.109375 to 0.109375
- doc_ids: int32 [65536], P('req'), may hold values from 0 to 512, never falling along the last dimension, each value on 1 to 32768 neighbouring positions
- page_owner: int32 [512], P('req'), may hold values from 0 to 31, as said below
- page_slot: int32 [512], P('req'), may hold values from 0 to 15
Outputs:
- layer_out: bfloat16 [65536, 1024], P('req')
- kv_cache: bfloat16 [512, 128, 2048], P('req', None, 'tp')
Inputs may be any that keep to these rules, and one draw needn't show every extreme that they name: `page_owner`: the pages of one index of req going to one owner number at most 1, and every owner receives exactly 16 pages, one for each of its slots.
All inputs are finite; a program needn't handle non-finite values.
Results may differ from a plain program's by a relative error of at most 0.015.
Values may be sent and summed in bfloat16 or wider, within the bound.
No kernel may reach another device: no remote copies, remote signals or barrier semaphores. Data moves between devices by JAX's collectives and lax.ppermute only.
A program may use at most 128 MiB of HBM per device.

v0:
```python
import math

import jax
import jax.numpy as jnp
from jax import lax
from jax.sharding import PartitionSpec as P

HEAD_DIM = 128
PERSIST = 16
SEG = 1024
PAGE = 128


norm_eps = 1e-05
unit_eps = 1e-06
big_negative = -1e30


def entering(shard, axis, combine, identity):
    devices, position = (lax.axis_size(axis), lax.axis_index(axis))
    everything = jax.tree.map(lambda part: lax.all_gather(part, axis), shard)
    start = jax.tree.map(
        lambda part, zero: jnp.broadcast_to(jnp.asarray(zero, part.dtype), part.shape),
        shard,
        identity,
    )

    def step(k, before):
        reached = k < position
        new = combine(before, jax.tree.map(lambda part: part[k], everything))
        return jax.tree.map(lambda a, b: jnp.where(reached, a, b), new, before)

    return lax.fori_loop(0, devices, step, start)


def rms_scale(values, gain):
    wide = values.astype(jnp.float32)
    return (
        wide
        * lax.rsqrt(jnp.mean(wide * wide, axis=-1, keepdims=True) + norm_eps)
        * gain.astype(jnp.float32)
    )


def unit_rows(values):
    wide = values.astype(jnp.float32)
    return (
        wide
        * lax.rsqrt(jnp.mean(wide * wide, axis=-1, keepdims=True) + unit_eps)
        / math.sqrt(wide.shape[-1])
    )


def attend(queries, key_rows, value_rows, docs, persist_keys, persist_values):
    scale = 1.0 / math.sqrt(queries.shape[-1])
    local = (
        jnp.einsum("thd,shd->hts", queries, key_rows, preferred_element_type=jnp.float32) * scale
    )
    order = jnp.arange(docs.shape[0])
    allowed = (order[None, :] <= order[:, None]) & (docs[None, :] == docs[:, None])
    local = jnp.where(allowed[None], local, big_negative)
    persist = (
        jnp.einsum("thd,phd->htp", queries, persist_keys, preferred_element_type=jnp.float32)
        * scale
    )
    peak = jnp.maximum(jnp.max(persist, axis=-1), jnp.max(local, axis=-1))
    weight_persist = jnp.exp(persist - peak[..., None])
    weight_local = jnp.exp(local - peak[..., None])
    total = jnp.sum(weight_persist, axis=-1) + jnp.sum(weight_local, axis=-1)
    probs_persist = (weight_persist / total[..., None]).astype(jnp.bfloat16)
    probs_local = (weight_local / total[..., None]).astype(jnp.bfloat16)
    return jnp.einsum(
        "htp,phd->thd", probs_persist, persist_values, preferred_element_type=jnp.float32
    ) + jnp.einsum("hts,shd->thd", probs_local, value_rows, preferred_element_type=jnp.float32)


def memory_block(carry, inputs):
    state, carried = carry
    q_unit, k_unit, value_rows, decay_log, docs = inputs
    value_wide = value_rows.astype(jnp.float32)
    cumul = jnp.cumsum(decay_log, axis=0)
    diff = cumul[:, None, :] - cumul[None, :, :]
    order = jnp.arange(docs.shape[0])
    allowed = ((order[None, :] <= order[:, None]) & (docs[None, :] == docs[:, None]))[:, :, None]
    decay = jnp.where(allowed, jnp.exp(jnp.where(allowed, diff, 0.0)), 0.0)
    inner = jnp.einsum("thd,shd->tsh", q_unit, k_unit, precision=lax.Precision.HIGHEST) * decay
    recall = jnp.einsum("tsh,shd->thd", inner, value_wide, precision=lax.Precision.HIGHEST)
    continues = (docs == carried).astype(jnp.float32)
    reach = jnp.exp(cumul) * continues[:, None]
    recall = (
        recall
        + jnp.einsum("thd,hde->the", q_unit, state, precision=lax.Precision.HIGHEST)
        * reach[:, :, None]
    )
    last_doc = docs[-1]
    keep = jnp.exp(cumul[-1][None, :] - cumul) * (docs == last_doc).astype(jnp.float32)[:, None]
    kept = jnp.exp(cumul[-1]) * (last_doc == carried).astype(jnp.float32)
    state_next = (
        jnp.einsum(
            "shd,she->hde", k_unit * keep[:, :, None], value_wide, precision=lax.Precision.HIGHEST
        )
        + state * kept[:, None, None]
    )
    return ((state_next, last_doc), recall)


def combine_maps(earlier, later):
    joins = jnp.logical_or(
        jnp.logical_or(earlier[3] == later[2], earlier[3] < 0), later[2] < 0
    ).astype(jnp.float32)
    carry_factor = later[0] * joins
    return (
        carry_factor * earlier[0],
        carry_factor[:, None, None] * earlier[1] + later[1],
        jnp.where(earlier[2] < 0, later[2], earlier[2]),
        jnp.where(later[3] < 0, earlier[3], later[3]),
    )


def place_pages(key3, value3, page_owner, page_slot):
    page_count = page_owner.shape[0]
    req_count = lax.axis_size("req")
    capacity = max(1, page_count // req_count)
    pages = jnp.stack([key3, value3], axis=2).reshape(page_count, -1)
    order = jnp.arange(page_count)
    same_owner = page_owner[:, None] == page_owner[None, :]
    rank = jnp.sum((same_owner & (order[:, None] < order[None, :])).astype(jnp.int32), axis=0)
    bucket = page_owner * capacity + rank
    targets = jnp.arange(req_count * capacity)
    routing = targets[:, None] == bucket[None, :]
    outgoing = jnp.dot(
        routing.astype(jnp.bfloat16), pages, preferred_element_type=jnp.float32
    ).astype(jnp.bfloat16)
    outgoing = outgoing.reshape(req_count, capacity, -1)
    codes = (jnp.sum(routing.astype(jnp.int32) * (page_slot[None, :] + 1), axis=1) - 1).astype(
        jnp.bfloat16
    )
    codes = codes.reshape(req_count, capacity)
    arrived, arrived_codes = (
        lax.all_to_all(outgoing, "req", split_axis=0, concat_axis=0, tiled=True),
        lax.all_to_all(codes, "req", split_axis=0, concat_axis=0, tiled=True),
    )
    wanted = (
        arrived_codes.reshape(-1).astype(jnp.float32)[None, :]
        == jnp.arange(page_count).astype(jnp.float32)[:, None]
    )
    cache = jnp.dot(
        wanted.astype(jnp.bfloat16),
        arrived.reshape(req_count * capacity, -1),
        preferred_element_type=jnp.float32,
    )
    return cache.astype(jnp.bfloat16).reshape(page_count, PAGE, -1)


def on_device(
    tokens,
    attn_gain,
    w_query,
    w_key,
    w_value,
    persist_key,
    persist_value,
    log_forget,
    mem_gain,
    w_out,
    ffn_gain,
    w_gate,
    w_up,
    w_down,
    doc_ids,
    page_owner,
    page_slot,
):
    tok_count = tokens.shape[0]
    heads_here = w_query.shape[1] // HEAD_DIM
    normed = rms_scale(tokens, attn_gain).astype(jnp.bfloat16)
    queries = jnp.dot(normed, w_query, preferred_element_type=jnp.float32).astype(jnp.bfloat16)
    key_rows = jnp.dot(normed, w_key, preferred_element_type=jnp.float32).astype(jnp.bfloat16)
    value_rows = jnp.dot(normed, w_value, preferred_element_type=jnp.float32).astype(jnp.bfloat16)
    shape3 = (tok_count, heads_here, HEAD_DIM)
    kv_cache = place_pages(
        key_rows.reshape(shape3), value_rows.reshape(shape3), page_owner, page_slot
    )
    blocks = tok_count // SEG
    shape4 = (blocks, SEG, heads_here, HEAD_DIM)
    q_unit = unit_rows(queries.reshape(shape3))
    k_unit = unit_rows(key_rows.reshape(shape3))
    doc_blocks = doc_ids.reshape(blocks, SEG)
    mem_rows = math.gcd(tok_count, 512)
    mem_blocks = tok_count // mem_rows
    mem_shape = (mem_blocks, mem_rows, heads_here, HEAD_DIM)
    start = (jnp.zeros((heads_here, HEAD_DIM, HEAD_DIM), jnp.float32), jnp.int32(-1))
    finish, recall = lax.scan(
        memory_block,
        start,
        (
            q_unit.reshape(mem_shape),
            k_unit.reshape(mem_shape),
            value_rows.reshape(mem_shape),
            log_forget.reshape(mem_blocks, mem_rows, heads_here),
            doc_ids.reshape(mem_blocks, mem_rows),
        ),
    )
    local_state = finish[0]
    recall = recall.reshape(shape3)
    cumul = jnp.cumsum(log_forget, axis=0)
    whole_doc = (doc_ids[0] == doc_ids[-1]).astype(jnp.float32)
    element = (
        jnp.exp(cumul[-1]) * whole_doc,
        local_state,
        doc_ids[0].astype(jnp.float32),
        doc_ids[-1].astype(jnp.float32),
    )
    identity = (
        jnp.ones((heads_here,), jnp.float32),
        jnp.zeros_like(local_state),
        jnp.float32(-1.0),
        jnp.float32(-1.0),
    )
    prefix = entering(element, "req", combine_maps, identity)
    continues = (doc_ids.astype(jnp.float32) == prefix[3]).astype(jnp.float32)
    reach = jnp.exp(cumul) * continues[:, None]
    recall = (
        recall
        + jnp.einsum("thd,hde->the", q_unit, prefix[1], precision=lax.Precision.HIGHEST)
        * reach[:, :, None]
    )
    persist_keys = persist_key.reshape(PERSIST, heads_here, HEAD_DIM)
    persist_values = persist_value.reshape(PERSIST, heads_here, HEAD_DIM)

    def attend_block(parts):
        return attend(parts[0], parts[1], parts[2], parts[3], persist_keys, persist_values)

    attended = lax.map(
        attend_block,
        (queries.reshape(shape4), key_rows.reshape(shape4), value_rows.reshape(shape4), doc_blocks),
    )
    memory_out = rms_scale(recall, mem_gain.reshape(heads_here, HEAD_DIM))
    heads_out = (
        (attended.reshape(shape3) + memory_out)
        .astype(jnp.bfloat16)
        .reshape(tok_count, heads_here * HEAD_DIM)
    )
    head_total = lax.psum(jnp.dot(heads_out, w_out, preferred_element_type=jnp.float32), "tp")
    resid = (tokens.astype(jnp.float32) + head_total).astype(jnp.bfloat16)
    normed_ffn = rms_scale(resid, ffn_gain).astype(jnp.bfloat16)
    gate_proj = jnp.dot(normed_ffn, w_gate, preferred_element_type=jnp.float32)
    up_proj = jnp.dot(normed_ffn, w_up, preferred_element_type=jnp.float32)
    hidden = (jax.nn.silu(gate_proj) * up_proj).astype(jnp.bfloat16)
    unit_total = lax.psum(
        jnp.dot(hidden, w_down, preferred_element_type=jnp.float32).astype(jnp.bfloat16), "tp"
    ).astype(jnp.float32)
    layer_out = (resid.astype(jnp.float32) + unit_total).astype(jnp.bfloat16)
    return (layer_out, kv_cache)


def solution(mesh):
    return jax.shard_map(
        on_device,
        mesh=mesh,
        in_specs=(
            P("req", None),
            P(),
            P(None, "tp"),
            P(None, "tp"),
            P(None, "tp"),
            P(None, "tp"),
            P(None, "tp"),
            P("req", "tp"),
            P("tp"),
            P("tp", None),
            P(),
            P(None, "tp"),
            P(None, "tp"),
            P("tp", None),
            P("req"),
            P("req"),
            P("req"),
        ),
        out_specs=(P("req", None), P("req", None, "tp")),
        check_vma=False,
    )
```

profile of v0, /device:TPU:32, one launch (start us, length us, event | category | flops | bytes accessed | tf_op | source)
XLA Modules:
  0.0 915.2 jit_solution(10726321676844413340)
XLA Ops:
  8.1 3.4 fusion.62
  11.5 3.6 multiply_reduce_fusion.1
  15.1 2.5 bitcast_reduce_fusion
  17.6 2.5 convolution_convert_fusion.3
  20.1 2.7 reshape.341
  22.8 2.9 copy.215
  26.6 2.7 reshape.340
  29.3 3.0 copy.213
  36.0 4.2 multiply_multiply_fusion
  40.2 113.1 %while.42 = (s32[]{:T(128)}, f32[2,128,128]{2,1,0:T(8,128)}, s32[]{:T(128)}, f32[4,512,2,128]{1,0,3,2:T(4,128)}, f32[4,512,2,128]{3,1,2,0:T(8,128)}, /*index=5*/...) while((s32[]{:T(128)}, f32[2,128,128]{2,1,0:T(8,128)}, ...), condition=%wide.region_12.13_spmd.clone, body=%wide.region_9.12_spmd.clone.sunk | while | flops 2016809984 | bytes 11492285 | solution.py:193
  40.3 3.0 fusion.150
  46.0 3.3 fusion.152
  53.8 2.5 convolution_add_fusion.2
  56.8 11.1 %dynamic_update_slice.12 = f32[4,512,2,128]{1,0,3,2:T(4,128)} dynamic-update-slice(f32[4,512,2,128]{1,0,3,2:T(4,128)} %get-tuple-element.758, f32[1,512,2,128]{1,0,3,2:T(1,128)S(1)} %copy.278, s32[]{:T(128)S(6)} %copy.291, s32[]{:T(128)} %constant.104.clone.1..sunk.1, s32[]{:T(128)} %constant.104.clone.1..sunk.1, s32[]{:T(128)} %constant.104.clone.1..sunk.1) | dynamic-update-slice | bytes 1048580 | tf_op jit(solution)/shard_map/while/body/jit(dynamic_update_index_in_dim)/dynamic_update_slice | solution.py:193
  68.5 3.0 fusion.150
  74.2 3.3 fusion.152
  82.0 2.6 convolution_add_fusion.2
  85.1 11.1 %dynamic_update_slice.12 = f32[4,512,2,128]{1,0,3,2:T(4,128)} dynamic-update-slice(f32[4,512,2,128]{1,0,3,2:T(4,128)} %get-tuple-element.758, f32[1,512,2,128]{1,0,3,2:T(1,128)S(1)} %copy.278, s32[]{:T(128)S(6)} %copy.291, s32[]{:T(128)} %constant.104.clone.1..sunk.1, s32[]{:T(128)} %constant.104.clone.1..sunk.1, s32[]{:T(128)} %constant.104.clone.1..sunk.1) | dynamic-update-slice | bytes 1048580 | tf_op jit(solution)/shard_map/while/body/jit(dynamic_update_index_in_dim)/dynamic_update_slice | solution.py:193
  96.8 3.0 fusion.150
  102.5 3.3 fusion.152
  110.3 2.6 convolution_add_fusion.2
  113.4 11.1 %dynamic_update_slice.12 = f32[4,512,2,128]{1,0,3,2:T(4,128)} dynamic-update-slice(f32[4,512,2,128]{1,0,3,2:T(4,128)} %get-tuple-element.758, f32[1,512,2,128]{1,0,3,2:T(1,128)S(1)} %copy.278, s32[]{:T(128)S(6)} %copy.291, s32[]{:T(128)} %constant.104.clone.1..sunk.1, s32[]{:T(128)} %constant.104.clone.1..sunk.1, s32[]{:T(128)} %constant.104.clone.1..sunk.1) | dynamic-update-slice | bytes 1048580 | tf_op jit(solution)/shard_map/while/body/jit(dynamic_update_index_in_dim)/dynamic_update_slice | solution.py:193
  125.0 3.0 fusion.150
  130.7 3.3 fusion.152
  138.5 2.6 convolution_add_fusion.2
  141.6 11.1 %dynamic_update_slice.12 = f32[4,512,2,128]{1,0,3,2:T(4,128)} dynamic-update-slice(f32[4,512,2,128]{1,0,3,2:T(4,128)} %get-tuple-element.758, f32[1,512,2,128]{1,0,3,2:T(1,128)S(1)} %copy.278, s32[]{:T(128)S(6)} %copy.291, s32[]{:T(128)} %constant.104.clone.1..sunk.1, s32[]{:T(128)} %constant.104.clone.1..sunk.1, s32[]{:T(128)} %constant.104.clone.1..sunk.1) | dynamic-update-slice | bytes 1048580 | tf_op jit(solution)/shard_map/while/body/jit(dynamic_update_index_in_dim)/dynamic_update_slice | solution.py:193
  153.4 3.0 reshape.322
  157.7 2.6 reshape.325
  163.5 3.7 copy.206
  167.2 3.7 copy.208
  172.1 64.1 %while.41 = (s32[]{:T(128)}, f32[2,1024,2,128]{1,0,3,2:T(2,128)}, bf16[2,1024,2,128]{3,1,2,0:T(8,128)(2,1)}, bf16[16,2,128]{2,0,1:T(8,128)(2,1)S(1)}, s32[2,1024...) while((s32[]{:T(128)}, f32[2,1024,2,128]{1,0,3,2:T(2,128)}, ...), condition=%wide.region_6.7_spmd, body=%wide.region_1.6_spmd.sunk | while | flops 1119318016 | bytes 39351420 | solution.py:234
  173.5 3.0 fusion.138
  179.9 4.3 fusion.142
  185.4 18.8 %dynamic_update_slice.11 = f32[2,1024,2,128]{1,0,3,2:T(2,128)} dynamic-update-slice(f32[2,1024,2,128]{1,0,3,2:T(2,128)} %get-tuple-element.723, f32[1,1024,2,128]{1,0,3,2:T(1,128)S(1)} %copy.275, s32[]{:T(128)S(6)} %copy.283, s32[]{:T(128)} %constant.104.clone.1..sunk, s32[]{:T(128)} %constant.104.clone.1..sunk, s32[]{:T(128)} %constant.104.clone.1..sunk) | dynamic-update-slice | bytes 2097156 | tf_op jit(solution)/shard_map/while/body/jit(dynamic_update_index_in_dim)/dynamic_update_slice | solution.py:234
  205.5 3.0 fusion.138
  211.9 4.3 fusion.142
  217.4 18.8 %dynamic_update_slice.11 = f32[2,1024,2,128]{1,0,3,2:T(2,128)} dynamic-update-slice(f32[2,1024,2,128]{1,0,3,2:T(2,128)} %get-tuple-element.723, f32[1,1024,2,128]{1,0,3,2:T(1,128)S(1)} %copy.275, s32[]{:T(128)S(6)} %copy.283, s32[]{:T(128)} %constant.104.clone.1..sunk, s32[]{:T(128)} %constant.104.clone.1..sunk, s32[]{:T(128)} %constant.104.clone.1..sunk) | dynamic-update-slice | bytes 2097156 | tf_op jit(solution)/shard_map/while/body/jit(dynamic_update_index_in_dim)/dynamic_update_slice | solution.py:234
  236.2 4.0 reshape.328
  240.2 2.7 reshape.332
  253.5 2.9 copy.220
  258.4 24.2 %all-gather.1 = f32[32,1,2]{2,1,0:T(1,128)} all-gather(f32[1,1,2]{2,1,0:T(1,128)S(1)} %bitcast.265), channel_id=1, replica_groups=mesh['req'=32,'tp'=4] {'req'}, dimensions={0}, use_global_device_ids=true | all-gather | bytes 264 | tf_op jit(solution)/shard_map/all_gather | solution.py:21
  287.5 60.4 %all-reduce.2 = (f32[32]{0:T(128)}, f32[32]{0:T(128)}) all-reduce(f32[32]{0:T(128)} %convert_dynamic-update-slice_fusion.1, f32[32]{0:T(128)} %convert_dynamic-update-slice_fusion), channel_id=1, replica_groups=mesh['req'=32,'tp'=4] {'req'}, use_global_device_ids=true, to_apply=%add | all-reduce | flops 64 | bytes 512
  347.9 255.1 %while.43 = (s32[]{:T(128)}, f32[2,128,128]{2,1,0:T(8,128)}, f32[]{:T(128)}, s32[]{:T(128)}, f32[32,2]{1,0:T(8,128)}, /*index=5*/f32[32]{0:T(128)}, f32[32,2,128...) while((s32[]{:T(128)}, f32[2,128,128]{2,1,0:T(8,128)}, ...), condition=%wide.region_16.17_spmd.clone, body=%wide.region_15.16_spmd.clone.sunk | while | flops 131087 | bytes 393486 | solution.py:33
  604.6 4.3 multiply_reduce_fusion
  610.0 4.5 fusion.98
  616.6 9.0 all-to-all-start
  626.9 3.7 copy.224
  630.6 3.7 copy.223
  634.4 5.8 pad_maximum_fusion
  640.2 2.6 reshape.336
  642.7 5.0 fusion.61
  648.2 6.8 reduce.10
  655.0 6.6 reshape.365
  661.6 114.8 %all-reduce.6.cloned.1.call-done = f32[2048,1024]{1,0:T(8,128)} async-done(((f32[2048,1024]{1,0:T(8,128)}), f32[2048,1024]{1,0:T(8,128)}) %all-reduce.6.cloned.1.call-update) | async-done | bytes 8388624 | tf_op jit(solution)/shard_map/psum | solution.py:244
  776.4 5.9 fusion.66
  784.3 5.1 fusion.78
  789.4 7.7 all-to-all-start.1
  797.3 10.8 %convolution_convert_fusion.2 = bf16[2048,1024]{1,0:T(8,128)(2,1)} fusion(bf16[704,1024]{1,0:T(8,128)(2,1)S(1)} %copy-done, f32[2048,704]{0,1:T(8,128)} %fusion.78, bf16[1024,704]{0,1:T(8,128)(2,1)S(1)} %copy-done.24, bf16[2048,1024]{1,0:T(8,128)(2,1)} %copy-done.1, f32[1024]{0:T(1024)S(1)} %copy-done.20, f32[2048]{0:T(1024)S(1)} %add_rsqrt_fusion.3), kind=kOutput, calls=%fused_computation.108 | convolution fusion | flops 5924716544 | bytes 17051648 | tf_op jit(solution)/shard_map/dot_general | solution.py:251
  808.5 43.1 %all-to-all-done.1 = bf16[32,2,32768]{2,1,0:T(2,128)(2,1)} async-done(((bf16[32,2,32768]{2,1,0:T(2,128)(2,1)}), bf16[32,2,32768]{2,1,0:T(2,128)(2,1)}, u32[]{:S(2)}, u32[]{:S(2)}) %all-to-all-start.1) | async-done | bytes 4194336 | tf_op jit(solution)/shard_map/all_to_all | solution.py:140
  851.6 19.9 %reshape.366 = bf16[32,1,65536]{2,1,0:T(2,128)(2,1)} reshape(bf16[32,2,32768]{2,1,0:T(2,128)(2,1)} %all-to-all-done.1) | data formatting | bytes 8388608
  871.5 8.0 convolution_convert_fusion.1
  879.5 2.0 copy.251
  881.5 19.4 %all-reduce.8.cloned.1.call-done = bf16[2048,1024]{1,0:T(8,128)(2,1)} async-done(((bf16[2048,1024]{1,0:T(8,128)(2,1)}), bf16[2048,1024]{1,0:T(8,128)(2,1)}) %all-reduce.8.cloned.1.call-update) | async-done | bytes 4194320 | tf_op jit(solution)/shard_map/psum | solution.py:250
  900.9 7.6 fusion.69
  (320 shorter events, 250.2 us)
Async XLA Ops:
  7.2 790.2 %copy-start = (bf16[704,1024]{1,0:T(8,128)(2,1)S(1)}, bf16[704,1024]{1,0:T(8,128)(2,1)}, u32[]{:S(2)}) copy-start(bf16[704,1024]{1,0:T(8,128)(2,1)} %param.36) | copy-start | bytes 4325380
  7.2 340.7 %all-gather.4.cloned.1.call-start = ((), (), s32[]{:S(2)}) async-start(), calls=%async_computation.4 | async-start | bytes 4325376 | tf_op jit(solution)/shard_map/all_gather | solution.py:21
  7.2 4.2 copy-start.2
  11.5 3.6 copy-start.25
  15.1 5.1 copy-start.5
  15.1 2.5 copy-start.26
  17.6 9.0 copy-start.3
  25.7 7.7 copy-start.7
  26.6 9.4 %copy-start.13 = (f32[2048,2]{0,1:T(2,128)}, f32[2048,2]{0,1:T(2,128)S(1)}, u32[]{:S(2)}) copy-start(f32[2048,2]{0,1:T(2,128)S(1)} %add_rsqrt_fusion.1) | copy-start | bytes 49156
  29.3 3.0 copy-start.17
  29.3 3.6 copy-start.16
  153.3 7.0 copy-start.8
  153.3 8.6 copy-start.6
  153.3 623.1 %all-reduce.6.cloned.1.call-start = ((), (), s32[]{:S(2)}) async-start(), calls=%async_computation.2 | async-start | bytes 16777216 | tf_op jit(solution)/shard_map/psum | solution.py:244
  161.9 9.0 copy-start.11
  163.5 8.7 copy-start.18
  163.5 8.7 copy-start.19
  242.9 361.7 %copy-start.14 = (f32[2048,2]{0,1:T(2,128)S(1)}, f32[2048,2]{0,1:T(2,128)}, u32[]{:S(2)}) copy-start(f32[2048,2]{0,1:T(2,128)} %copy-done.13) | copy-start | bytes 49156
  249.8 0.6 copy-start.15
  603.0 6.0 copy-start.10
  603.0 6.0 copy-start.21
  608.9 1.0 copy-start.12
  614.5 0.7 copy-start.27
  614.5 0.8 copy-start.28
  614.5 12.4 %copy-start.9 = (bf16[2048,256]{0,1:T(8,128)(2,1)S(1)}, bf16[2048,256]{0,1:T(8,128)(2,1)}, u32[]{:S(2)}) copy-start(bf16[2048,256]{0,1:T(8,128)(2,1)} %convolution_convert_fusion.3) | copy-start | bytes 3145732
  614.5 16.2 %copy-start.4 = (bf16[2048,256]{0,1:T(8,128)(2,1)S(1)}, bf16[2048,256]{0,1:T(8,128)(2,1)}, u32[]{:S(2)}) copy-start(bf16[2048,256]{0,1:T(8,128)(2,1)} %copy-done.3) | copy-start | bytes 3145732
  615.2 0.5 copy-start.22
  616.6 172.9 %all-to-all-start = ((bf16[32,1,1]{2,1,0:T(2,128)(2,1)}), bf16[32,1,1]{2,1,0:T(2,128)(2,1)S(1)}, u32[]{:S(2)}, u32[]{:S(2)}) async-start(bf16[32,1,1]{2,1,0:T(2,128)(2,1)} %copy.222), calls=%async_computation | async-start | bytes 32768 | tf_op jit(solution)/shard_map/all_to_all | solution.py:141
  661.6 122.7 %copy-start.20 = (f32[1024]{0:T(1024)S(1)}, f32[1024]{0:T(1024)}, u32[]{:S(2)}) copy-start(f32[1024]{0:T(1024)} %convert_element_type.185) | copy-start | bytes 12292
  661.6 122.7 %copy-start.23 = (bf16[1024,704]{0,1:T(8,128)(2,1)S(1)}, bf16[1024,704]{0,1:T(8,128)(2,1)}, u32[]{:S(2)}) copy-start(bf16[1024,704]{0,1:T(8,128)(2,1)} %param.34) | copy-start | bytes 4325380
  782.3 2.0 copy-start.1
  789.4 7.9 copy-start.24
  789.4 62.2 %all-to-all-start.1 = ((bf16[32,2,32768]{2,1,0:T(2,128)(2,1)}), bf16[32,2,32768]{2,1,0:T(2,128)(2,1)}, u32[]{:S(2)}, u32[]{:S(2)}) async-start(bf16[32,2,32768]{2,1,0:T(2,128)(2,1)} %reshape.365), calls=%async_computation.1 | async-start | bytes 8388608 | tf_op jit(solution)/shard_map/all_to_all | solution.py:140
  797.1 103.8 %all-reduce.8.cloned.1.call-start = ((), (), s32[]{:S(2)}) async-start(), calls=%async_computation.3 | async-start | bytes 8388608 | tf_op jit(solution)/shard_map/psum | solution.py:250
Sparse Core Ops, SparseCore 0:
  153.5 48.0 all-gather.3
  614.6 161.7 all-reduce.5
  808.3 92.5 all-reduce.7
where the time goes:
time: 932 us; the launch traced here: 915 us
  local copies, waits for them, and re-layouts  271 us (29%)
  waiting for transfers between devices  177 us (19%)
  other arithmetic  156 us (17%)
  matrix products  107 us (11%)
  loops' own time  86.5 us (9%)
  blocking collectives  84.5 us (9%)
  starting transfers between devices  17 us (2%)
  between operations  15.5 us (2%)
    psum x1, waiting for transfers between devices, on_device(): lax.psum(jnp.dot(heads_out, w_out, preferred_element_type=jnp.float32), '...  115 us
    another operation x1, loops' own time, entering(): return lax.fori_loop(0, devices, step, start)  81.6 us
    dynamic_slice x64, local copies, waits for them, and re-layouts, step(): new = combine(before, jax.tree.map(lambda part: part[k], everything))  79.4 us
    unnamed x1, blocking collectives  60.4 us
    select_n x32, other arithmetic, step(): return jax.tree.map(lambda a, b: jnp.where(reached, a, b), new, before)  54.3 us
    dynamic_update_slice x8, local copies, waits for them, and re-layouts, on_device(): lax.scan(memory_block, start, (q_unit.reshape(mem_shape), k_unit.reshape(...  46.6 us
    all_to_all x1, waiting for transfers between devices, place_pages(): lax.all_to_all(outgoing, 'req', split_axis=0, concat_axis=0, tiled=True)  43.1 us
    mul x32, other arithmetic, combine_maps(): carry_factor = later[0] * joins  39.9 us
  transfers between devices with their start and end apart: 5, of which 3 were waited for; matrix products, arithmetic and copies ran while one was open for 22% of the time, Pallas kernels for 0%

commit v1 on v0

v1 whole, which is shorter than its diff:
```python
import math

import jax
import jax.numpy as jnp
from jax import lax
from jax.experimental import pallas as pl
from jax.experimental.pallas import tpu as pltpu
from jax.sharding import PartitionSpec as P

HD = 128
SEG = 1024
PAGE = 128
CH = 256
ROWS = 256
F32 = jnp.float32
BF = jnp.bfloat16
HI = lax.Precision.HIGHEST
ANY = pl.ANY


def rms(x, eps):
    return x * lax.rsqrt(jnp.mean(x * x, axis=-1, keepdims=True) + eps)


def dot(a, b):
    return jnp.dot(a, b, preferred_element_type=F32)


def dot_t(a, b):
    return lax.dot_general(a, b, (((1,), (1,)), ((), ())), preferred_element_type=F32)


def dot_l(a, b):
    return lax.dot_general(a, b, (((0,), (0,)), ((), ())), preferred_element_type=F32)


def tri(n, lower=True):
    r = lax.broadcasted_iota(jnp.int32, (n, n), 0)
    c = lax.broadcasted_iota(jnp.int32, (n, n), 1)
    return (r >= c) if lower else (r <= c)


def split3(x):
    hi = x.astype(BF).astype(F32)
    mid = (x - hi).astype(BF).astype(F32)
    return hi, mid, x - hi - mid


def project_kernel(tok, gain, wq, wk, wv, col, q_out, kv_out, ku_out, min_out, pay_out, st, misc):
    i = pl.program_id(0)

    @pl.when(i == 0)
    def _():
        st[...] = jnp.zeros_like(st)
        misc[...] = jnp.full_like(misc, -1.0)
        misc[0:2, :] = jnp.zeros((2, 128), F32)

    n = (rms(tok[...].astype(F32), 1e-5) * gain[...].astype(F32)).astype(BF)
    q_out[...] = dot(n, wq[...]).astype(BF)
    k = dot(n, wk[...]).astype(BF)
    v = dot(n, wv[...]).astype(BF)
    mask = tri(CH).astype(F32)
    for h in range(2):
        s = slice(h * HD, (h + 1) * HD)
        kv_out[:, 2 * h * HD : (2 * h + 1) * HD] = k[:, s]
        kv_out[:, (2 * h + 1) * HD : (2 * h + 2) * HD] = v[:, s]
    for j in range(tok.shape[0] // CH):
        r = slice(j * CH, (j + 1) * CH)
        info = col[r, :]
        cum = jnp.dot(mask, info, precision=HI, preferred_element_type=F32)
        end = cum[CH - 1 : CH, :]
        doc = info[:, 0:1]
        last = info[CH - 1 : CH, 0:1]
        same = (doc == last).astype(F32)
        last_row = jnp.broadcast_to(last, (1, 128))
        cont = (last_row == misc[2:3, :]).astype(F32)
        for h in range(2):
            s = slice(h * HD, (h + 1) * HD)
            ku = rms(k[r, s].astype(F32), 1e-6) * (1.0 / math.sqrt(HD))
            ku_out[r, s] = ku.astype(BF)
            end_h = end[:, 1 + h : 2 + h]
            w = jnp.exp(end_h - cum[:, 1 + h : 2 + h]) * same
            add = dot_l((ku * w).astype(BF), v[r, s])
            end_row = jnp.broadcast_to(end_h, (1, 128))
            old = st[h]
            min_out[j, h] = old
            st[h] = old * (jnp.exp(end_row) * cont) + add
            misc[h : h + 1, :] = misc[h : h + 1, :] + end_row
        misc[2:3, :] = last_row

    @pl.when(i == pl.num_programs(0) - 1)
    def _():
        write_payload(pay_out, st, misc[0:1, :], misc[1:2, :], misc[2:3, :])


def write_payload(out, st, l0, l1, last):
    for h in range(2):
        out[h * HD : (h + 1) * HD, :] = st[h].astype(BF)
    hi = jnp.floor(last * (1.0 / 256.0))
    rows = [*split3(l0), *split3(l1), hi, last - hi * 256.0]
    out[2 * HD : 2 * HD + 8, :] = jnp.concatenate(rows, axis=0).astype(BF)


def read_payload(ref, j):
    s = ref[j, 2 * HD : 2 * HD + 8, :].astype(F32)
    l0 = s[0:1] + s[1:2] + s[2:3]
    l1 = s[3:4] + s[4:5] + s[5:6]
    return l0, l1, s[6:7] * 256.0 + s[7:8]


def project(tokens, gain, wq, wk, wv, col):
    t, d = tokens.shape
    tile = 512
    n = t // tile
    c = tile // CH
    full = lambda a: pl.BlockSpec(a.shape, lambda i: (0, 0))
    row = lambda w: pl.BlockSpec((tile, w), lambda i: (i, 0))
    return pl.pallas_call(
        project_kernel,
        grid=(n,),
        in_specs=[row(d), full(gain), full(wq), full(wk), full(wv), row(8)],
        out_specs=[
            row(256),
            row(512),
            row(256),
            pl.BlockSpec((c, 2, HD, HD), lambda i: (i, 0, 0, 0)),
            pl.BlockSpec((264, 128), lambda i: (0, 0)),
        ],
        out_shape=[
            jax.ShapeDtypeStruct((t, 256), BF),
            jax.ShapeDtypeStruct((t, 512), BF),
            jax.ShapeDtypeStruct((t, 256), BF),
            jax.ShapeDtypeStruct((t // CH, 2, HD, HD), F32),
            jax.ShapeDtypeStruct((264, 128), BF),
        ],
        scratch_shapes=[pltpu.VMEM((2, HD, HD), F32), pltpu.VMEM((8, 128), F32)],
        name="project",
    )(tokens, gain, wq, wk, wv, col)


def combine_kernel(place, got, e_out, info_out, pay_out, st):
    g = place[0]
    st[...] = jnp.zeros_like(st)
    e_out[...] = jnp.zeros_like(e_out)
    cur = jnp.full((1, 128), -1.0, F32)
    t0 = t1 = jnp.zeros((1, 128), F32)
    i0, i1, il = t0, t1, cur
    for j in range(8):
        @pl.when(g == j)
        def _():
            e_out[...] = st[...]

        here = g == j
        i0, i1, il = jnp.where(here, t0, i0), jnp.where(here, t1, i1), jnp.where(here, cur, il)
        l0, l1, last = read_payload(got, j)
        cont = (cur == last).astype(F32)
        for h, l in ((0, l0), (1, l1)):
            st[h] = st[h] * (jnp.exp(l) * cont) + got[j, h * HD : (h + 1) * HD, :].astype(F32)
        t0, t1, cur = t0 + l0, t1 + l1, last
    info_out[...] = jnp.concatenate([i0, i1, il, jnp.zeros((5, 128), F32)], axis=0)
    write_payload(pay_out, st, t0, t1, cur)


def combine(place, got):
    vm = pl.BlockSpec(memory_space=pltpu.VMEM)
    return pl.pallas_call(
        combine_kernel,
        in_specs=[pl.BlockSpec(memory_space=pltpu.SMEM), vm],
        out_specs=[vm, vm, vm],
        out_shape=[
            jax.ShapeDtypeStruct((2, HD, HD), F32),
            jax.ShapeDtypeStruct((8, 128), F32),
            jax.ShapeDtypeStruct((264, 128), BF),
        ],
        scratch_shapes=[pltpu.VMEM((2, HD, HD), F32)],
        name="combine",
    )(place, got)


def attend_kernel(q, k, v, pk, pv, col, row, out):
    scale = 1.0 / math.sqrt(HD)
    c = scale * math.log2(math.e)
    mask = tri(CH)
    for i in range(SEG // CH):
        r = slice(i * CH, (i + 1) * CH)
        qi = q[r, :]
        doc = col[r, 0:1]
        sp = dot_t(qi, pk[...])
        sd = dot_t(qi, k[r, :])
        sd = jnp.where(mask & (doc == row[0:1, r]), sd, -1e30)
        m = jnp.maximum(jnp.max(sp, axis=-1, keepdims=True), jnp.max(sd, axis=-1, keepdims=True))
        if i:
            e = slice(0, i * CH)
            so = dot_t(qi, k[e, :])
            so = jnp.where(doc == row[0:1, e], so, -1e30)
            m = jnp.maximum(m, jnp.max(so, axis=-1, keepdims=True))
        wp = jnp.exp2((sp - m) * c)
        wd = jnp.exp2((sd - m) * c)
        total = jnp.sum(wp, axis=-1, keepdims=True) + jnp.sum(wd, axis=-1, keepdims=True)
        acc = dot(wp.astype(BF), pv[...]) + dot(wd.astype(BF), v[r, :])
        if i:
            wo = jnp.exp2((so - m) * c)
            total = total + jnp.sum(wo, axis=-1, keepdims=True)
            acc = acc + dot(wo.astype(BF), v[e, :])
        out[r, :] = acc / total


def attend(q, kv, pk, pv, col, row, seg):
    return pl.pallas_call(
        attend_kernel,
        grid=(2,),
        in_specs=[
            pl.BlockSpec((SEG, HD), lambda h: (seg, h)),
            pl.BlockSpec((SEG, HD), lambda h: (seg, 2 * h)),
            pl.BlockSpec((SEG, HD), lambda h: (seg, 2 * h + 1)),
            pl.BlockSpec((16, HD), lambda h: (0, h)),
            pl.BlockSpec((16, HD), lambda h: (0, h)),
            pl.BlockSpec((SEG, 8), lambda h: (seg, 0)),
            pl.BlockSpec((8, SEG), lambda h: (0, seg)),
        ],
        out_specs=pl.BlockSpec((SEG, HD), lambda h: (0, h)),
        out_shape=jax.ShapeDtypeStruct((SEG, 2 * HD), F32),
        name="attend",
    )(q, kv, kv, pk, pv, col, row)


def recall_kernel(half, place, bound, q, ku, kv, mi, e1, info, got, col, row, rows, at0, at1, gain, out, pst, pdoc):
    b = pl.program_id(0)
    chunk = 2 * b + half

    @pl.when(b == 0)
    def _():
        x, g = place[1], place[0]
        st = [jnp.zeros((HD, HD), F32)] * 2
        cur = jnp.full((1, 128), -1.0, F32)
        pst[...] = jnp.zeros_like(pst)
        il = cur
        for j in range(4):
            here = x == j
            il = jnp.where(here, cur, il)
            for h in range(2):
                pst[h] = jnp.where(here, st[h], pst[h])
            l0, l1, last = read_payload(got, j)
            cont = (cur == last).astype(F32)
            for h, l in ((0, l0), (1, l1)):
                st[h] = st[h] * (jnp.exp(l) * cont) + got[j, h * HD : (h + 1) * HD, :].astype(F32)
            cur = last
        glast = info[2:3, :]
        first = g == 0
        ok = jnp.where(first, 1.0, (il == glast).astype(F32))
        for h in range(2):
            pst[h] = pst[h] * (jnp.exp(info[h : h + 1, :]) * ok) + e1[h]
        pdoc[0:1, :] = jnp.where(first, il, glast)

    mask = tri(CH)
    c_col = jnp.dot(mask.astype(F32), col[...], precision=HI, preferred_element_type=F32)
    c_row = jnp.dot(row[...], tri(CH, False).astype(F32), precision=HI, preferred_element_type=F32)
    pos = lax.broadcasted_iota(jnp.int32, rows.shape, 1)
    pre = jnp.sum(jnp.where(pos < chunk * CH, rows[...], 0.0), axis=1, keepdims=True)
    doc = col[:, 0:1]
    pdoc_row = pdoc[0:1, :]
    carried = jnp.where(chunk == 0, pdoc_row, bound[chunk])
    joined = (carried == pdoc_row).astype(F32)
    live = (doc == carried[:, 0:1]).astype(F32)
    ok = mask & (doc == row[0:1, :])
    for h in range(2):
        s = slice(h * HD, (h + 1) * HD)
        qh = q[:, s]
        cc = c_col[:, 1 + h : 2 + h]
        dec = jnp.exp(jnp.where(ok, cc - c_row[1 + h : 2 + h, :], -1e30))
        inner = (dot_t(qh, ku[:, s]) * dec).astype(BF)
        rec = dot(inner, kv[:, (2 * h + 1) * HD : (2 * h + 2) * HD])
        f = jnp.exp(jnp.broadcast_to(pre[1 + h : 2 + h, :], (1, 128))) * joined
        m = mi[0, h] + pst[h] * f
        rec = rec + dot(qh, m.astype(BF)) * (jnp.exp(cc) * live)
        qw = qh.astype(F32)
        rec = rec * (lax.rsqrt(jnp.mean(qw * qw, axis=-1, keepdims=True) + 1e-6) * (1.0 / math.sqrt(HD)))
        at = jnp.where(chunk < SEG // CH, at0[:, s], at1[:, s])
        out[0, :, s] = (at + rms(rec, 1e-5) * gain[:, s]).astype(BF)


def recall(half, place, bound, q, ku, kv, mi, e1, info, got, col, row, at0, at1, gain):
    import functools

    ch = lambda w: pl.BlockSpec((CH, w), lambda b, p, d: (2 * b + half, 0))
    full = lambda a: pl.BlockSpec(a.shape, lambda b, p, d: (0,) * a.ndim)
    per = SEG // CH
    gs = pltpu.PrefetchScalarGridSpec(
        num_scalar_prefetch=2,
        grid=(4,),
        in_specs=[
            ch(256),
            ch(256),
            ch(512),
            pl.BlockSpec((1, 2, HD, HD), lambda b, p, d: (2 * b + half, 0, 0, 0)),
            full(e1),
            full(info),
            full(got),
            ch(8),
            pl.BlockSpec((8, CH), lambda b, p, d: (0, 2 * b + half)),
            full(row),
            pl.BlockSpec((CH, 256), lambda b, p, d: (jnp.minimum(2 * b + half, per - 1), 0)),
            pl.BlockSpec((CH, 256), lambda b, p, d: (jnp.maximum(2 * b + half - per, 0), 0)),
            full(gain),
        ],
        out_specs=pl.BlockSpec((1, CH, 256), lambda b, p, d: (lax.rem(b - p[2] + 4, 4), 0, 0)),
        scratch_shapes=[pltpu.VMEM((2, HD, HD), F32), pltpu.VMEM((8, 128), F32)],
    )
    return pl.pallas_call(
        functools.partial(recall_kernel, half),
        grid_spec=gs,
        out_shape=jax.ShapeDtypeStruct((4, CH, 256), BF),
        name="recall",
    )(place, bound, q, ku, kv, mi, e1, info, got, col, row, row, at0, at1, gain)


def ffn_kernel(place, tok, gain, h0, h1, h2, h3, *rest):
    own = rest[0:4]
    gu = (rest[4:7], rest[7:10])
    do = (rest[10:13], rest[13:16])
    out, wg, wu, wd, wo, sem = rest[16:]
    core = place[3]
    copies = []

    def copy(src, dst):
        c = pltpu.make_async_copy(src, dst, sem.at[len(copies)])
        c.start()
        copies.append(c)
        return c

    outs, ups, downs = [], [], []
    hh, hd, ho = 512, 352, 128
    outs.append([copy(own[3], wo.at[0])])
    for d in range(3):
        outs.append([copy(do[p][d].at[pl.ds(hd, ho), :], wo.at[d + 1, pl.ds((core if p == 0 else 1 - core) * ho, ho), :]) for p in range(2)])
    for d in range(4):
        if d == 0:
            ups.append([copy(own[0], wg.at[0]), copy(own[1], wu.at[0])])
            downs.append([copy(own[2], wd.at[0])])
            continue
        u, w = [], []
        for p in range(2):
            at = core if p == 0 else 1 - core
            u.append(copy(gu[p][d - 1].at[0], wg.at[d, pl.ds(at * hh, hh), :]))
            u.append(copy(gu[p][d - 1].at[1], wu.at[d, pl.ds(at * hh, hh), :]))
            w.append(copy(do[p][d - 1].at[pl.ds(0, hd), :], wd.at[d, pl.ds(at * hd, hd), :]))
        ups.append(u)
        downs.append(w)
    acc = tok[...].astype(F32)
    for d, h in enumerate((h0, h1, h2, h3)):
        for c in outs[d]:
            c.wait()
        acc = acc + dot(h[...], wo[d])
    resid = acc.astype(BF).astype(F32)
    n = (rms(resid, 1e-5) * gain[...].astype(F32)).astype(BF)
    acc = resid
    for d in range(4):
        for c in ups[d]:
            c.wait()
        g = dot(n, wg[d])
        u = dot(n, wu[d])
        hid = (g / (1.0 + jnp.exp(-g)) * u).astype(BF)
        for c in downs[d]:
            c.wait()
        acc = acc + dot(hid, wd[d])
    out[...] = acc.astype(BF)


def ffn(half, place, tokens, gain, heads, own, gu, gux, do, dox):
    d = tokens.shape[1]
    full = lambda a: pl.BlockSpec(a.shape, lambda i, p: (0,) * a.ndim)
    anys = pl.BlockSpec(memory_space=ANY)
    ws = [*own, *gu, *gux, *do, *dox]
    gs = pltpu.PrefetchScalarGridSpec(
        num_scalar_prefetch=1,
        grid=(1,),
        in_specs=[pl.BlockSpec((ROWS, d), lambda i, p: (2 * p[2] + half, 0)), full(gain)]
        + [full(h) for h in heads]
        + [anys] * len(ws),
        out_specs=pl.BlockSpec((ROWS, d), lambda i, p: (0, 0)),
        scratch_shapes=[
            pltpu.VMEM((4, 1024, 704), BF),
            pltpu.VMEM((4, 1024, 704), BF),
            pltpu.VMEM((4, 704, 1024), BF),
            pltpu.VMEM((4, 256, 1024), BF),
            pltpu.SemaphoreType.DMA((28,)),
        ],
    )
    return pl.pallas_call(
        ffn_kernel,
        grid_spec=gs,
        out_shape=jax.ShapeDtypeStruct((ROWS, d), BF),
        name="ffn",
    )(place, tokens, gain, *heads, *ws)


def dispatch_kernel(owner, pages, codes, out, sem):
    copies = []
    n = pages.shape[0]
    for p in range(n):
        copies.append(pltpu.make_async_copy(pages.at[p], out.at[owner[p], pl.ds(0, PAGE), :], sem.at[p]))
    for o in range(out.shape[0]):
        copies.append(pltpu.make_async_copy(codes.at[o], out.at[o, pl.ds(PAGE, 8), :], sem.at[n + o]))
    for c in copies:
        c.start()
    for c in copies:
        c.wait()


def dispatch(owner, pages, codes, count):
    anys = pl.BlockSpec(memory_space=ANY)
    return pl.pallas_call(
        dispatch_kernel,
        in_specs=[pl.BlockSpec(memory_space=pltpu.SMEM), anys, anys],
        out_specs=anys,
        out_shape=jax.ShapeDtypeStruct((count, PAGE + 8, pages.shape[2]), BF),
        scratch_shapes=[pltpu.SemaphoreType.DMA((pages.shape[0] + count,))],
        name="dispatch",
    )(owner, pages, codes)


def place_kernel(source, got, out, sem):
    copies = [
        pltpu.make_async_copy(got.at[source[s], pl.ds(0, PAGE), :], out.at[s], sem.at[s])
        for s in range(out.shape[0])
    ]
    for c in copies:
        c.start()
    for c in copies:
        c.wait()


def place_pages(source, got, count):
    anys = pl.BlockSpec(memory_space=ANY)
    return pl.pallas_call(
        place_kernel,
        in_specs=[pl.BlockSpec(memory_space=pltpu.SMEM), anys],
        out_specs=anys,
        out_shape=jax.ShapeDtypeStruct((count, PAGE, got.shape[2]), BF),
        scratch_shapes=[pltpu.SemaphoreType.DMA((count,))],
        name="place",
    )(source, got)


def join_kernel(place, *refs):
    pieces, out, sem = refs[:10], refs[10], refs[11]
    y = place[2]
    copies = []
    for half in range(2):
        own, a, b, lo, hi = pieces[5 * half : 5 * half + 5]
        for src, d, off, n in ((own, 0, 0, ROWS), (a, 3, 0, ROWS), (b, 1, 0, ROWS), (lo, 2, 0, ROWS // 2), (hi, 2, ROWS // 2, ROWS // 2)):
            at = lax.rem(y + d, 4) * (2 * ROWS) + half * ROWS + off
            copies.append(pltpu.make_async_copy(src, out.at[pl.ds(at, n), :], sem.at[len(copies)]))
    for c in copies:
        c.start()
    for c in copies:
        c.wait()


def join(place, pieces):
    anys = pl.BlockSpec(memory_space=ANY)
    return pl.pallas_call(
        join_kernel,
        in_specs=[pl.BlockSpec(memory_space=pltpu.SMEM)] + [anys] * 10,
        out_specs=anys,
        out_shape=jax.ShapeDtypeStruct((8 * ROWS, pieces[0].shape[1]), BF),
        scratch_shapes=[pltpu.SemaphoreType.DMA((10,))],
        name="join",
    )(place, *pieces)


def on_device(
    tokens, attn_gain, w_query, w_key, w_value, persist_key, persist_value, log_forget, mem_gain,
    w_out, ffn_gain, w_gate, w_up, w_down, doc_ids, page_owner, page_slot,
):
    count = tokens.shape[0]
    reqs = lax.axis_size("req")
    req, y = lax.axis_index("req"), lax.axis_index("tp")
    core = req % 2
    place = jnp.stack([req % 8, req // 8, y, core]).astype(jnp.int32)
    shift = lambda a, d: lax.ppermute(a, "tp", [(i, (i + d) % 4) for i in range(4)])
    swap = lambda a: lax.ppermute(a, "req", [(i, i ^ 1) for i in range(reqs)])

    cut = lambda w: lax.dynamic_slice_in_dim(w, core * (w.shape[0] // 2), w.shape[0] // 2, 0)
    gu_half = jnp.stack([cut(w_gate), cut(w_up)])
    do_half = jnp.concatenate([cut(w_down), cut(w_out)])
    do = [shift(do_half, d) for d in (1, 2, 3)]
    gu = [shift(gu_half, d) for d in (1, 2, 3)]

    doc = doc_ids.astype(F32)
    row = jnp.concatenate([doc[None], log_forget.T, jnp.zeros((5, count), F32)])
    col = jnp.concatenate([doc[:, None], log_forget, jnp.zeros((count, 5), F32)], axis=1)
    bound = jnp.concatenate([jnp.full((1,), -1.0, F32), doc[CH - 1 : -1 : CH]])

    q, kv, ku, mi, pay = project(tokens, attn_gain[None], w_query, w_key, w_value, col)

    group8 = [[x * 8 + k for k in range(8)] for x in range(reqs // 8)]
    group4 = [[x * 8 + k for x in range(reqs // 8)] for k in range(8)]
    spread = lambda a, n, g: lax.all_to_all(
        jnp.broadcast_to(a[None], (n, *a.shape)), "req", 0, 0, tiled=True, axis_index_groups=g
    )
    got8 = spread(pay, 8, group8)

    at0 = attend(q, kv, persist_key, persist_value, col, row, 0)
    e1, info, pay4 = combine(place, got8)
    got4 = spread(pay4, 4, group4)
    at1 = attend(q, kv, persist_key, persist_value, col, row, 1)

    pages = kv.reshape(count // PAGE, PAGE, 512)
    hit = page_owner[None, :] == jnp.arange(reqs)[:, None]
    code = jnp.sum(jnp.where(hit, page_slot[None, :] + 1, 0), axis=1).astype(BF)
    codes = jnp.broadcast_to(code[:, None, None], (reqs, 8, 512))
    outgoing = dispatch(page_owner, pages, codes, reqs)
    arrived = lax.all_to_all(outgoing, "req", 0, 0, tiled=True)

    gux = [swap(a) for a in gu]
    dox = [swap(a) for a in do]
    gain = mem_gain[None]
    pieces = []
    for half in range(2):
        out = recall(half, place, bound, q, ku, kv, mi, e1, info, got4, col, row, at0, at1, gain)
        heads = [out[0]] + [shift(out[d], d) for d in (1, 2, 3)]
        own = ffn(half, place, tokens, ffn_gain[None], heads, (w_gate, w_up, w_down, w_out), gu, gux, do, dox)
        a, b = shift(own, 1), shift(own, -1)
        lo = shift(a[: ROWS // 2], 1)
        hi = shift(b[ROWS // 2 :], -1)
        pieces += [own, a, b, lo, hi]
    layer_out = join(place, pieces)

    slots = arrived[:, PAGE, 0].astype(F32)
    wanted = slots[None, :] == (jnp.arange(count // PAGE) + 1).astype(F32)[:, None]
    source = jnp.sum(jnp.where(wanted, jnp.arange(reqs)[None, :], 0), axis=1).astype(jnp.int32)
    kv_cache = place_pages(source, arrived, count // PAGE)
    return layer_out, kv_cache


def solution(mesh):
    return jax.shard_map(
        on_device,
        mesh=mesh,
        in_specs=(
            P("req", None), P(), P(None, "tp"), P(None, "tp"), P(None, "tp"), P(None, "tp"), P(None, "tp"),
            P("req", "tp"), P("tp"), P("tp", None), P(), P(None, "tp"), P(None, "tp"), P("tp", None),
            P("req"), P("req"), P("req"),
        ),
        out_specs=(P("req", None), P("req", None, "tp")),
        check_vma=False,
    )
```

time: 932 us -> 503 us (0.54); the launches traced: 915 us -> 502 us
  Pallas kernels: 0 us -> 334 us
  local copies, waits for them, and re-layouts: 271 us -> 35.8 us
  other arithmetic: 156 us -> 5.39 us
  matrix products: 107 us -> 0 us
  waiting for transfers between devices: 177 us -> 75.7 us
  loops' own time: 86.5 us -> 0 us
  blocking collectives: 84.5 us -> 0 us
  starting transfers between devices: 17 us -> 49.7 us
  between operations: 15.5 us -> 1.22 us
    pallas_call x0 -> x11, Pallas kernels: none -> 334 us  [the longest x1 129 us: join(): pl.pallas_call(join_kernel, in_specs=[pl.BlockSpec(memory_space=pltpu.SME...]
    psum x2 -> x0, waiting for transfers between devices: 134 us -> none  [the longest x1 115 us: on_device(): lax.psum(jnp.dot(heads_out, w_out, preferred_element_type=jnp.float32), '...]
    dot_general x33 -> x0, matrix products: 107 us -> none  [the longest x4 13.4 us: memory_block(): jnp.einsum('tsh,shd->thd', inner, value_wide, precision=lax.Precision.HIG...]
    another operation x3 -> x0, loops' own time: 86.5 us -> none  [the longest x1 81.6 us: entering(): return lax.fori_loop(0, devices, step, start)]
    dynamic_update_slice x12 -> x0, local copies, waits for them, and re-layouts: 85.8 us -> none  [the longest x8 46.6 us: on_device(): lax.scan(memory_block, start, (q_unit.reshape(mem_shape), k_unit.reshape(...]
    dynamic_slice x70 -> x2, local copies, waits for them, and re-layouts: 83.6 us -> 0.07 us  [on_device(): lax.dynamic_slice_in_dim(w, core * (w.shape[0] // 2), w.shape[0] // 2, 0)]
    ppermute x0 -> x26, waiting for transfers between devices: none -> 75.7 us  [the longest x20 75.7 us: on_device(): lax.ppermute(a, 'tp', [(i, (i + d) % 4) for i in range(4)])]
    unnamed x1 -> x0, blocking collectives: 60.4 us -> none
  transfers between devices with their start and end apart: 5 -> 29, of which waited for: 3 -> 8; matrix products, arithmetic and copies ran while one was open for 22% -> 7% of each run, Pallas kernels for 0% -> 54%
where the time goes in v1:
time: 503 us; the launch traced here: 502 us
  Pallas kernels  334 us (66%)
  waiting for transfers between devices  75.7 us (15%)
  starting transfers between devices  49.7 us (10%)
  local copies, waits for them, and re-layouts  35.8 us (7%)
  other arithmetic  5.39 us (1%)
    pallas_call x1, Pallas kernels, join(): pl.pallas_call(join_kernel, in_specs=[pl.BlockSpec(memory_space=pltpu.SME...  129 us
    ppermute x20, waiting for transfers between devices, on_device(): lax.ppermute(a, 'tp', [(i, (i + d) % 4) for i in range(4)])  75.7 us
    pallas_call x1, Pallas kernels, dispatch(): pl.pallas_call(dispatch_kernel, in_specs=[pl.BlockSpec(memory_space=pltpu...  73.7 us
    pallas_call x1, Pallas kernels, place_pages(): pl.pallas_call(place_kernel, in_specs=[pl.BlockSpec(memory_space=pltpu.SM...  65.4 us
    ppermute x20, starting transfers between devices, on_device(): lax.ppermute(a, 'tp', [(i, (i + d) % 4) for i in range(4)])  30.4 us
    pallas_call x2, Pallas kernels, ffn(): pl.pallas_call(ffn_kernel, grid_spec=gs, out_shape=jax.ShapeDtypeStruct((...  22.8 us
    pallas_call x2, Pallas kernels, recall(): pl.pallas_call(functools.partial(recall_kernel, half), grid_spec=gs, out_...  15.8 us
    pallas_call x1, Pallas kernels, project(): pl.pallas_call(project_kernel, grid=(n,), in_specs=[row(d), full(gain), f...  12.7 us
  transfers between devices with their start and end apart: 29, of which 8 were waited for; matrix products, arithmetic and copies ran while one was open for 7% of the time, Pallas kernels for 54%

profile of v1, /device:TPU:32, one launch (start us, length us, event | category | flops | bytes accessed | tf_op | source)
XLA Modules:
  0.0 501.9 jit_solution(5068549425260066437)
XLA Ops:
  0.6 1.4 dynamic-slice_bitcast_fusion
  2.1 1.2 pad_maximum_fusion
  3.3 3.0 collective-permute-start.5
  6.4 0.6 collective-permute-start.4
  7.0 1.0 collective-permute-start.3
  8.0 0.6 broadcast_in_dim.71.gain
  8.7 1.3 copy.55.col
  10.0 12.7 %project.1 = (bf16[2048,256]{1,0:T(8,128)(2,1)}, bf16[2048,512]{1,0:T(8,128)(2,1)}, bf16[2048,256]{1,0:T(8,128)(2,1)}, f32[8,2,128,128]{3,2,1,0:T(8,128)}, bf16[264,128]{1,0:T(8,128)(2,1)}) custom-call(bf16[2048,1024]{1,0:T(8,128)(2,1)} %tok.5, bf16[1,1024]{1,0:T(2,128)(2,1)} %broadcast_in_dim.71.gain, bf16[1024,256]{1,0:T(8,128)(2,1)} %wq.1, ...), custom_call_target="tpu_custom_call" | custom-call | tf_op jit(solution)/shard_map/project/pallas_call | solution.py:118
  22.8 1.8 broadcast_in_dim.74
  24.6 5.4 %all-to-all-start = ((bf16[8,264,128]{2,1,0:T(8,128)(2,1)}), bf16[8,264,128]{2,1,0:T(8,128)(2,1)S(1)}, u32[]{:S(2)}, u32[]{:S(2)}) async-start(bf16[8,264,128]{2,1,0:T(8,128)(2,1)} %broadcast_in_dim.74), calls=%async_computation | async-start | bytes 1081344 | tf_op jit(solution)/shard_map/all_to_all | solution.py:499
  30.0 0.7 maximum_maximum_fusion.1.row.rows
  30.8 6.4 %attend.3.at1 = f32[1024,256]{1,0:T(8,128)} custom-call(bf16[2048,256]{1,0:T(8,128)(2,1)} %get-tuple-element.10.q, bf16[2048,512]{1,0:T(8,128)(2,1)} %get-tuple-element.12.k.v.kv, bf16[2048,512]{1,0:T(8,128)(2,1)} %get-tuple-element.12.k.v.kv, bf16[16,256]{1,0:T(8,128)(2,1)} %pk.3, bf16[16,256]{1,0:T(8,128)(2,1)} %pv.3, f32[2048,8]{1,0:T(8,128)} %copy.55.col, ...), custom_call_target="tpu_custom_call" | custom-call | tf_op jit(solution)/shard_map/attend/pallas_call | solution.py:209
  37.2 6.4 %attend.2.at0 = f32[1024,256]{1,0:T(8,128)} custom-call(bf16[2048,256]{1,0:T(8,128)(2,1)} %get-tuple-element.10.q, bf16[2048,512]{1,0:T(8,128)(2,1)} %get-tuple-element.12.k.v.kv, bf16[2048,512]{1,0:T(8,128)(2,1)} %get-tuple-element.12.k.v.kv, bf16[16,256]{1,0:T(8,128)(2,1)} %pk.3, bf16[16,256]{1,0:T(8,128)(2,1)} %pv.3, f32[2048,8]{1,0:T(8,128)} %copy.55.col, ...), custom_call_target="tpu_custom_call" | custom-call | tf_op jit(solution)/shard_map/attend/pallas_call | solution.py:209
  43.5 0.7 pad_add_fusion.place
  44.2 0.8 copy-done.8
  45.0 1.9 combine.1
  46.9 1.6 broadcast_in_dim.75
  48.6 4.3 all-to-all-start.1
  53.0 0.8 broadcast_in_dim.81.codes
  53.8 73.7 %dispatch.1 = bf16[32,136,512]{2,1,0:T(8,128)(2,1)} custom-call(s32[16]{0:T(128)} %owner.1, bf16[16,128,512]{2,1,0:T(8,128)(2,1)} %bitcast.29, bf16[32,8,512]{2,1,0:T(8,128)(2,1)} %broadcast_in_dim.81.codes), custom_call_target="tpu_custom_call" | custom-call | tf_op jit(solution)/shard_map/dispatch/pallas_call | solution.py:412
  127.5 0.7 pad_maximum_fusion.2.bound
  128.1 0.7 copy-done.7
  128.8 8.0 %all-to-all-start.2 = ((bf16[32,136,512]{2,1,0:T(8,128)(2,1)}), bf16[32,136,512]{2,1,0:T(8,128)(2,1)}, u32[]{:S(2)}, u32[]{:S(2)}) async-start(bf16[32,136,512]{2,1,0:T(8,128)(2,1)} %dispatch.1), calls=%async_computation.2 | async-start | bytes 8912896 | tf_op jit(solution)/shard_map/all_to_all | solution.py:514
  136.8 8.0 %recall.2 = bf16[4,256,256]{2,1,0:T(8,128)(2,1)} custom-call(s32[4]{0:T(128)} %pad_add_fusion.place, f32[8]{0:T(128)} %pad_maximum_fusion.2.bound, bf16[2048,256]{1,0:T(8,128)(2,1)} %get-tuple-element.10.q, bf16[2048,256]{1,0:T(8,128)(2,1)} %get-tuple-element.11.ku, bf16[2048,512]{1,0:T(8,128)(2,1)} %get-tuple-element.12.k.v.kv, ...), custom_call_target="tpu_custom_call" | custom-call | tf_op jit(solution)/shard_map/recall/pallas_call | solution.py:309
  144.8 1.9 slice_bitcast_fusion.4
  146.7 2.3 collective-permute-start.2
  149.1 1.8 collective-permute-start.1
  150.8 4.0 collective-permute-done.2.h3
  154.9 2.1 collective-permute-start
  157.0 1.8 collective-permute-start.11
  158.9 2.6 collective-permute-done.h1
  161.5 1.8 collective-permute-start.10
  163.3 36.5 %collective-permute-done.11.rest_12_ = bf16[480,1024]{1,0:T(8,128)(2,1)S(1)} collective-permute-done((bf16[480,1024]{1,0:T(8,128)(2,1)S(1)}, bf16[480,1024]{1,0:T(8,128)(2,1)S(1)}, u32[]{:S(2)}, u32[]{:S(2)}) %collective-permute-start.11) | collective-permute-done | bytes 983072 | tf_op jit(solution)/shard_map/ppermute | solution.py:481
  200.9 14.6 %collective-permute-done.9.rest_10_ = bf16[480,1024]{1,0:T(8,128)(2,1)S(1)} collective-permute-done((bf16[480,1024]{1,0:T(8,128)(2,1)S(1)}, bf16[480,1024]{1,0:T(8,128)(2,1)S(1)}, u32[]{:S(2)}, u32[]{:S(2)}) %collective-permute-start.9) | collective-permute-done | bytes 983072 | tf_op jit(solution)/shard_map/ppermute | solution.py:481
  215.6 1.0 copy-done.4
  217.0 7.8 %recall.3 = bf16[4,256,256]{2,1,0:T(8,128)(2,1)} custom-call(s32[4]{0:T(128)} %pad_add_fusion.place, f32[8]{0:T(128)} %pad_maximum_fusion.2.bound, bf16[2048,256]{1,0:T(8,128)(2,1)} %get-tuple-element.10.q, bf16[2048,256]{1,0:T(8,128)(2,1)} %get-tuple-element.11.ku, bf16[2048,512]{1,0:T(8,128)(2,1)} %get-tuple-element.12.k.v.kv, ...), custom_call_target="tpu_custom_call" | custom-call | tf_op jit(solution)/shard_map/recall/pallas_call | solution.py:309
  224.9 1.9 slice_bitcast_fusion
  226.8 2.1 collective-permute-start.21
  228.9 1.0 collective-permute-start.19
  229.9 2.6 copy.59.rest_0_
  232.4 1.6 copy.60.rest_1_
  234.0 0.6 broadcast_in_dim.70.gain
  234.6 2.6 copy.61.rest_4_
  237.2 2.6 copy.62.rest_5_
  239.8 2.6 copy.63.rest_6_
  242.4 2.6 copy.66.rest_9_
  244.9 2.6 copy.65.rest_8_
  247.5 2.6 copy.64.rest_7_
  250.1 11.4 %ffn.2.refs_0_ = bf16[256,1024]{1,0:T(8,128)(2,1)} custom-call(s32[4]{0:T(128)} %pad_add_fusion.place, bf16[2048,1024]{1,0:T(8,128)(2,1)} %tok.5, bf16[1,1024]{1,0:T(2,128)(2,1)} %broadcast_in_dim.70.gain, bf16[256,256]{1,0:T(8,128)(2,1)} %get-tuple-element.25.h0, bf16[256,256]{1,0:T(8,128)(2,1)} %copy-done.18, bf16[256,256]{1,0:T(8,128)(2,1)} %collective-permute-done.1.h2, ...), custom_call_target="tpu_custom_call" | custom-call | tf_op jit(solution)/shard_map/ffn/pallas_call | solution.py:389
  261.5 2.6 collective-permute-start.16
  264.5 0.6 copy-done.19
  265.1 11.4 %ffn.3.refs_5_ = bf16[256,1024]{1,0:T(8,128)(2,1)} custom-call(s32[4]{0:T(128)} %pad_add_fusion.place, bf16[2048,1024]{1,0:T(8,128)(2,1)} %tok.5, bf16[1,1024]{1,0:T(2,128)(2,1)} %broadcast_in_dim.70.gain, bf16[256,256]{1,0:T(8,128)(2,1)} %get-tuple-element.21.h0, bf16[256,256]{1,0:T(8,128)(2,1)} %collective-permute-done.19.h1, ...), custom_call_target="tpu_custom_call" | custom-call | tf_op jit(solution)/shard_map/ffn/pallas_call | solution.py:389
  276.5 3.0 collective-permute-start.23
  279.5 3.3 collective-permute-start.18
  282.9 9.3 %collective-permute-done.23.refs_7_ = bf16[256,1024]{1,0:T(8,128)(2,1)S(1)} collective-permute-done((bf16[256,1024]{1,0:T(8,128)(2,1)}, bf16[256,1024]{1,0:T(8,128)(2,1)S(1)}, u32[]{:S(2)}, u32[]{:S(2)}) %collective-permute-start.23) | collective-permute-done | bytes 524320 | tf_op jit(solution)/shard_map/ppermute | solution.py:481
  292.2 3.7 collective-permute-start.25
  296.0 1.7 collective-permute-done.18.refs_4_
  297.7 3.7 collective-permute-done.17.refs_3_
  301.4 3.2 collective-permute-done.24.refs_8_
  304.7 0.7 copy-done.16
  305.4 128.9 %join.1 = bf16[2048,1024]{1,0:T(8,128)(2,1)} custom-call(s32[4]{0:T(128)} %pad_add_fusion.place, bf16[256,1024]{1,0:T(8,128)(2,1)} %ffn.2.refs_0_, bf16[256,1024]{1,0:T(8,128)(2,1)} %copy-done.10, bf16[256,1024]{1,0:T(8,128)(2,1)} %copy-done.9, bf16[128,1024]{1,0:T(8,128)(2,1)} %copy-done.14, bf16[128,1024]{1,0:T(8,128)(2,1)} %copy-done.13, ...), custom_call_target="tpu_custom_call" | custom-call | tf_op jit(solution)/shard_map/join/pallas_call | solution.py:462
  434.3 1.2 fusion
  435.5 0.8 select_reduce_fusion.source
  436.2 65.4 %place.1 = bf16[16,128,512]{2,1,0:T(8,128)(2,1)} custom-call(s32[16]{0:T(128)} %select_reduce_fusion.source, bf16[32,136,512]{2,1,0:T(8,128)(2,1)} %all-to-all-done.2.got), custom_call_target="tpu_custom_call" | custom-call | tf_op jit(solution)/shard_map/place/pallas_call | solution.py:435
  (96 shorter events, 2.7 us)
Async XLA Ops:
  2.1 5.9 %copy-start.22 = (bf16[1024]{0:T(1024)(128)(2,1)S(1)}, bf16[1024]{0:T(1024)(128)(2,1)}, u32[]{:S(2)}) copy-start(bf16[1024]{0:T(1024)(128)(2,1)} %param.18) | copy-start | bytes 6148
  2.1 6.5 %copy-start.21 = (s32[2048]{0:T(1024)S(1)}, s32[2048]{0:T(1024)}, u32[]{:S(2)}) copy-start(s32[2048]{0:T(1024)} %param.31) | copy-start | bytes 24580
  2.1 6.5 %copy-start.20 = (f32[2048,2]{0,1:T(2,128)S(1)}, f32[2048,2]{0,1:T(2,128)}, u32[]{:S(2)}) copy-start(f32[2048,2]{0,1:T(2,128)} %param.24) | copy-start | bytes 49156
  3.3 196.6 %collective-permute-start.5 = (bf16[2,512,704]{1,2,0:T(8,128)(2,1)}, bf16[2,512,704]{1,2,0:T(8,128)(2,1)}, u32[]{:S(2)}, u32[]{:S(2)}) collective-permute-start(bf16[2,512,704]{1,2,0:T(8,128)(2,1)} %pad_maximum_fusion), channel_id=1, source_target_pairs={{0,3},{1,0},{2,1},{3,2},{4,7},{5,4},{6,5},{7,6},{8,11},{9,8},{10,9... | collective-permute-start | bytes 4325384 | tf_op jit(solution)/shard_map/ppermute | solution.py:481
  6.4 194.1 %collective-permute-start.4 = (bf16[2,512,704]{1,2,0:T(8,128)(2,1)}, bf16[2,512,704]{1,2,0:T(8,128)(2,1)}, u32[]{:S(2)}, u32[]{:S(2)}) collective-permute-start(bf16[2,512,704]{1,2,0:T(8,128)(2,1)} %pad_maximum_fusion), channel_id=1, source_target_pairs={{0,2},{1,3},{2,0},{3,1},{4,6},{5,7},{6,4},{7,5},{8,10},{9,11},{10,... | collective-permute-start | bytes 4325384 | tf_op jit(solution)/shard_map/ppermute | solution.py:481
  7.0 193.5 %collective-permute-start.3 = (bf16[2,512,704]{1,2,0:T(8,128)(2,1)}, bf16[2,512,704]{1,2,0:T(8,128)(2,1)}, u32[]{:S(2)}, u32[]{:S(2)}) collective-permute-start(bf16[2,512,704]{1,2,0:T(8,128)(2,1)} %pad_maximum_fusion), channel_id=1, source_target_pairs={{0,1},{1,2},{2,3},{3,0},{4,5},{5,6},{6,7},{7,4},{8,9},{9,10},{10,1... | collective-permute-start | bytes 4325384 | tf_op jit(solution)/shard_map/ppermute | solution.py:481
  24.6 19.6 %all-to-all-start = ((bf16[8,264,128]{2,1,0:T(8,128)(2,1)}), bf16[8,264,128]{2,1,0:T(8,128)(2,1)S(1)}, u32[]{:S(2)}, u32[]{:S(2)}) async-start(bf16[8,264,128]{2,1,0:T(8,128)(2,1)} %broadcast_in_dim.74), calls=%async_computation | async-start | bytes 1081344 | tf_op jit(solution)/shard_map/all_to_all | solution.py:499
  37.2 7.0 %copy-start.25 = (s32[16]{0:T(128)S(1)}, s32[16]{0:T(128)}, u32[]{:S(2)}) copy-start(s32[16]{0:T(128)} %param.33) | copy-start | bytes 196
  37.2 15.7 %copy-start.24 = (s32[16]{0:T(128)S(1)}, s32[16]{0:T(128)}, u32[]{:S(2)}) copy-start(s32[16]{0:T(128)} %owner.1) | copy-start | bytes 196
  44.2 0.8 copy-start.8
  48.6 79.6 %all-to-all-start.1 = ((bf16[4,264,128]{2,1,0:T(8,128)(2,1)}), bf16[4,264,128]{2,1,0:T(8,128)(2,1)S(1)}, u32[]{:S(2)}, u32[]{:S(2)}) async-start(bf16[4,264,128]{2,1,0:T(8,128)(2,1)} %broadcast_in_dim.75), calls=%async_computation.1 | async-start | bytes 540672 | tf_op jit(solution)/shard_map/all_to_all | solution.py:499
  128.1 0.7 copy-start.7
  128.8 305.4 %all-to-all-start.2 = ((bf16[32,136,512]{2,1,0:T(8,128)(2,1)}), bf16[32,136,512]{2,1,0:T(8,128)(2,1)}, u32[]{:S(2)}, u32[]{:S(2)}) async-start(bf16[32,136,512]{2,1,0:T(8,128)(2,1)} %dispatch.1), calls=%async_computation.2 | async-start | bytes 8912896 | tf_op jit(solution)/shard_map/all_to_all | solution.py:514
  136.8 12.2 %copy-start.5 = (bf16[256,1024]{1,0:T(8,128)(2,1)S(1)}, bf16[256,1024]{1,0:T(8,128)(2,1)}, u32[]{:S(2)}) copy-start(bf16[256,1024]{1,0:T(8,128)(2,1)} %rest_3_.3) | copy-start | bytes 1572868
  144.8 4.2 copy-start
  146.7 8.2 %collective-permute-start.2 = (bf16[256,256]{1,0:T(8,128)(2,1)S(1)}, bf16[256,256]{1,0:T(8,128)(2,1)S(1)}, u32[]{:S(2)}, u32[]{:S(2)}) collective-permute-start(bf16[256,256]{1,0:T(8,128)(2,1)S(1)} %get-tuple-element.22), channel_id=1, source_target_pairs={{0,3},{1,0},{2,1},{3,2},{4,7},{5,4},{6,5},{7,6},{8,11},{9,8},{10,9... | collective-permute-start | bytes 393224 | tf_op jit(solution)/shard_map/ppermute | solution.py:481
  149.1 7.9 %collective-permute-start.1 = (bf16[256,256]{1,0:T(8,128)(2,1)S(1)}, bf16[256,256]{1,0:T(8,128)(2,1)}, u32[]{:S(2)}, u32[]{:S(2)}) collective-permute-start(bf16[256,256]{1,0:T(8,128)(2,1)S(1)} %get-tuple-element.23), channel_id=1, source_target_pairs={{0,2},{1,3},{2,0},{3,1},{4,6},{5,7},{6,4},{7,5},{8,10},{9,11},{10,... | collective-permute-start | bytes 393224 | tf_op jit(solution)/shard_map/ppermute | solution.py:481
  154.9 70.0 %copy-start.17 = (bf16[256,256]{1,0:T(8,128)(2,1)}, bf16[256,256]{1,0:T(8,128)(2,1)S(1)}, u32[]{:S(2)}) copy-start(bf16[256,256]{1,0:T(8,128)(2,1)S(1)} %collective-permute-done.2.h3) | copy-start | bytes 393220
  154.9 6.6 %collective-permute-start = (bf16[256,256]{1,0:T(8,128)(2,1)S(1)}, bf16[256,256]{1,0:T(8,128)(2,1)S(1)}, u32[]{:S(2)}, u32[]{:S(2)}) collective-permute-start(bf16[256,256]{1,0:T(8,128)(2,1)S(1)} %get-tuple-element.24), channel_id=1, source_target_pairs={{0,1},{1,2},{2,3},{3,0},{4,5},{5,6},{6,7},{7,4},{8,9},{9,10},{10,1... | collective-permute-start | bytes 393224 | tf_op jit(solution)/shard_map/ppermute | solution.py:481
  157.0 42.8 %collective-permute-start.11 = (bf16[480,1024]{1,0:T(8,128)(2,1)S(1)}, bf16[480,1024]{1,0:T(8,128)(2,1)S(1)}, u32[]{:S(2)}, u32[]{:S(2)}) collective-permute-start(bf16[480,1024]{1,0:T(8,128)(2,1)S(1)} %pad_maximum_fusion.1), channel_id=1, source_target_pairs={{0,3},{1,0},{2,1},{3,2},{4,7},{5,4},{6,5},{7,6},{8,11},{9,8},{10,9... | collective-permute-start | bytes 2949128 | tf_op jit(solution)/shard_map/ppermute | solution.py:481
  161.5 63.4 %copy-start.18 = (bf16[256,256]{1,0:T(8,128)(2,1)}, bf16[256,256]{1,0:T(8,128)(2,1)S(1)}, u32[]{:S(2)}) copy-start(bf16[256,256]{1,0:T(8,128)(2,1)S(1)} %collective-permute-done.h1) | copy-start | bytes 393220
  161.5 38.3 %collective-permute-start.10 = (bf16[480,1024]{1,0:T(8,128)(2,1)S(1)}, bf16[480,1024]{1,0:T(8,128)(2,1)S(1)}, u32[]{:S(2)}, u32[]{:S(2)}) collective-permute-start(bf16[480,1024]{1,0:T(8,128)(2,1)S(1)} %pad_maximum_fusion.1), channel_id=1, source_target_pairs={{0,2},{1,3},{2,0},{3,1},{4,6},{5,7},{6,4},{7,5},{8,10},{9,11},{10,... | collective-permute-start | bytes 2949128 | tf_op jit(solution)/shard_map/ppermute | solution.py:481
  199.8 25.1 %copy-start.1 = (bf16[480,1024]{1,0:T(8,128)(2,1)}, bf16[480,1024]{1,0:T(8,128)(2,1)S(1)}, u32[]{:S(2)}) copy-start(bf16[480,1024]{1,0:T(8,128)(2,1)S(1)} %collective-permute-done.11.rest_12_) | copy-start | bytes 2949124
  199.8 15.7 %collective-permute-start.9 = (bf16[480,1024]{1,0:T(8,128)(2,1)S(1)}, bf16[480,1024]{1,0:T(8,128)(2,1)S(1)}, u32[]{:S(2)}, u32[]{:S(2)}) collective-permute-start(bf16[480,1024]{1,0:T(8,128)(2,1)S(1)} %pad_maximum_fusion.1), channel_id=1, source_target_pairs={{0,1},{1,2},{2,3},{3,0},{4,5},{5,6},{6,7},{7,4},{8,9},{9,10},{10,1... | collective-permute-start | bytes 2949128 | tf_op jit(solution)/shard_map/ppermute | solution.py:481
  199.8 25.1 %copy-start.2 = (bf16[480,1024]{1,0:T(8,128)(2,1)}, bf16[480,1024]{1,0:T(8,128)(2,1)S(1)}, u32[]{:S(2)}) copy-start(bf16[480,1024]{1,0:T(8,128)(2,1)S(1)} %collective-permute-done.10.rest_11_) | copy-start | bytes 2949124
  199.8 15.7 %collective-permute-start.14 = (bf16[480,1024]{1,0:T(8,128)(2,1)S(1)}, bf16[480,1024]{1,0:T(8,128)(2,1)S(1)}, u32[]{:S(2)}, u32[]{:S(2)}) collective-permute-start(bf16[480,1024]{1,0:T(8,128)(2,1)S(1)} %collective-permute-done.11.rest_12_), channel_id=1, source_target_pairs={{0,4},{4,0},{8,12},{12,8},{16,20},{20,16},{24,28},{28,24},{32,36},... | collective-permute-start | bytes 2949128 | tf_op jit(solution)/shard_map/ppermute | solution.py:482
  199.9 26.9 %collective-permute-start.8 = (bf16[2,512,704]{1,2,0:T(8,128)(2,1)}, bf16[2,512,704]{1,2,0:T(8,128)(2,1)}, u32[]{:S(2)}, u32[]{:S(2)}) collective-permute-start(bf16[2,512,704]{1,2,0:T(8,128)(2,1)} %collective-permute-done.5), channel_id=1, source_target_pairs={{0,4},{4,0},{8,12},{12,8},{16,20},{20,16},{24,28},{28,24},{32,36},... | collective-permute-start | bytes 4325384 | tf_op jit(solution)/shard_map/ppermute | solution.py:482
  200.4 28.5 %collective-permute-start.7 = (bf16[2,512,704]{1,2,0:T(8,128)(2,1)}, bf16[2,512,704]{1,2,0:T(8,128)(2,1)}, u32[]{:S(2)}, u32[]{:S(2)}) collective-permute-start(bf16[2,512,704]{1,2,0:T(8,128)(2,1)} %collective-permute-done.4), channel_id=1, source_target_pairs={{0,4},{4,0},{8,12},{12,8},{16,20},{20,16},{24,28},{28,24},{32,36},... | collective-permute-start | bytes 4325384 | tf_op jit(solution)/shard_map/ppermute | solution.py:482
  200.5 28.4 %collective-permute-start.6 = (bf16[2,512,704]{1,2,0:T(8,128)(2,1)}, bf16[2,512,704]{1,2,0:T(8,128)(2,1)}, u32[]{:S(2)}, u32[]{:S(2)}) collective-permute-start(bf16[2,512,704]{1,2,0:T(8,128)(2,1)} %collective-permute-done.3), channel_id=1, source_target_pairs={{0,4},{4,0},{8,12},{12,8},{16,20},{20,16},{24,28},{28,24},{32,36},... | collective-permute-start | bytes 4325384 | tf_op jit(solution)/shard_map/ppermute | solution.py:482
  215.5 9.4 %copy-start.3 = (bf16[480,1024]{1,0:T(8,128)(2,1)}, bf16[480,1024]{1,0:T(8,128)(2,1)S(1)}, u32[]{:S(2)}) copy-start(bf16[480,1024]{1,0:T(8,128)(2,1)S(1)} %collective-permute-done.9.rest_10_) | copy-start | bytes 2949124
  215.5 34.6 %collective-permute-start.13 = (bf16[480,1024]{1,0:T(8,128)(2,1)S(1)}, bf16[480,1024]{1,0:T(8,128)(2,1)}, u32[]{:S(2)}, u32[]{:S(2)}) collective-permute-start(bf16[480,1024]{1,0:T(8,128)(2,1)S(1)} %collective-permute-done.10.rest_11_), channel_id=1, source_target_pairs={{0,4},{4,0},{8,12},{12,8},{16,20},{20,16},{24,28},{28,24},{32,36},... | collective-permute-start | bytes 2949128 | tf_op jit(solution)/shard_map/ppermute | solution.py:482
  215.5 1.0 copy-start.4
  216.6 33.5 %collective-permute-start.12 = (bf16[480,1024]{1,0:T(8,128)(2,1)S(1)}, bf16[480,1024]{1,0:T(8,128)(2,1)}, u32[]{:S(2)}, u32[]{:S(2)}) collective-permute-start(bf16[480,1024]{1,0:T(8,128)(2,1)S(1)} %collective-permute-done.9.rest_10_), channel_id=1, source_target_pairs={{0,4},{4,0},{8,12},{12,8},{16,20},{20,16},{24,28},{28,24},{32,36},... | collective-permute-start | bytes 2949128 | tf_op jit(solution)/shard_map/ppermute | solution.py:482
  226.8 5.6 %copy-start.6 = (bf16[1024,704]{0,1:T(8,128)(2,1)S(1)}, bf16[1024,704]{0,1:T(8,128)(2,1)}, u32[]{:S(2)}) copy-start(bf16[1024,704]{0,1:T(8,128)(2,1)} %param.29) | copy-start | bytes 4325380
  226.8 37.6 %collective-permute-start.21 = (bf16[256,256]{1,0:T(8,128)(2,1)}, bf16[256,256]{1,0:T(8,128)(2,1)S(1)}, u32[]{:S(2)}, u32[]{:S(2)}) collective-permute-start(bf16[256,256]{1,0:T(8,128)(2,1)} %get-tuple-element.18), channel_id=1, source_target_pairs={{0,3},{1,0},{2,1},{3,2},{4,7},{5,4},{6,5},{7,6},{8,11},{9,8},{10,9... | collective-permute-start | bytes 393224 | tf_op jit(solution)/shard_map/ppermute | solution.py:481
  228.9 35.5 %collective-permute-start.20 = (bf16[256,256]{1,0:T(8,128)(2,1)}, bf16[256,256]{1,0:T(8,128)(2,1)}, u32[]{:S(2)}, u32[]{:S(2)}) collective-permute-start(bf16[256,256]{1,0:T(8,128)(2,1)} %get-tuple-element.19), channel_id=1, source_target_pairs={{0,2},{1,3},{2,0},{3,1},{4,6},{5,7},{6,4},{7,5},{8,10},{9,11},{10,... | collective-permute-start | bytes 393224 | tf_op jit(solution)/shard_map/ppermute | solution.py:481
  228.9 35.5 %collective-permute-start.19 = (bf16[256,256]{1,0:T(8,128)(2,1)}, bf16[256,256]{1,0:T(8,128)(2,1)}, u32[]{:S(2)}, u32[]{:S(2)}) collective-permute-start(bf16[256,256]{1,0:T(8,128)(2,1)} %get-tuple-element.20), channel_id=1, source_target_pairs={{0,1},{1,2},{2,3},{3,0},{4,5},{5,6},{6,7},{7,4},{8,9},{9,10},{10,1... | collective-permute-start | bytes 393224 | tf_op jit(solution)/shard_map/ppermute | solution.py:481
  232.4 1.6 copy-start.23
  261.5 18.0 %collective-permute-start.16 = (bf16[256,1024]{1,0:T(8,128)(2,1)}, bf16[256,1024]{1,0:T(8,128)(2,1)S(1)}, u32[]{:S(2)}, u32[]{:S(2)}) collective-permute-start(bf16[256,1024]{1,0:T(8,128)(2,1)} %ffn.2.refs_0_), channel_id=1, source_target_pairs={{0,3},{1,0},{2,1},{3,2},{4,7},{5,4},{6,5},{7,6},{8,11},{9,8},{10,9... | collective-permute-start | bytes 1572872 | tf_op jit(solution)/shard_map/ppermute | solution.py:481
  264.2 18.7 %collective-permute-start.15 = (bf16[256,1024]{1,0:T(8,128)(2,1)}, bf16[256,1024]{1,0:T(8,128)(2,1)S(1)}, u32[]{:S(2)}, u32[]{:S(2)}) collective-permute-start(bf16[256,1024]{1,0:T(8,128)(2,1)} %ffn.2.refs_0_), channel_id=1, source_target_pairs={{0,1},{1,2},{2,3},{3,0},{4,5},{5,6},{6,7},{7,4},{8,9},{9,10},{10,1... | collective-permute-start | bytes 1572872 | tf_op jit(solution)/shard_map/ppermute | solution.py:481
  264.5 0.6 copy-start.19
  276.5 15.7 %collective-permute-start.23 = (bf16[256,1024]{1,0:T(8,128)(2,1)}, bf16[256,1024]{1,0:T(8,128)(2,1)S(1)}, u32[]{:S(2)}, u32[]{:S(2)}) collective-permute-start(bf16[256,1024]{1,0:T(8,128)(2,1)} %ffn.3.refs_5_), channel_id=1, source_target_pairs={{0,3},{1,0},{2,1},{3,2},{4,7},{5,4},{6,5},{7,6},{8,11},{9,8},{10,9... | collective-permute-start | bytes 1572872 | tf_op jit(solution)/shard_map/ppermute | solution.py:481
  279.5 16.4 %collective-permute-start.22 = (bf16[256,1024]{1,0:T(8,128)(2,1)}, bf16[256,1024]{1,0:T(8,128)(2,1)S(1)}, u32[]{:S(2)}, u32[]{:S(2)}) collective-permute-start(bf16[256,1024]{1,0:T(8,128)(2,1)} %ffn.3.refs_5_), channel_id=1, source_target_pairs={{0,1},{1,2},{2,3},{3,0},{4,5},{5,6},{6,7},{7,4},{8,9},{9,10},{10,1... | collective-permute-start | bytes 1572872 | tf_op jit(solution)/shard_map/ppermute | solution.py:481
  279.5 25.1 %copy-start.9 = (bf16[256,1024]{1,0:T(8,128)(2,1)}, bf16[256,1024]{1,0:T(8,128)(2,1)S(1)}, u32[]{:S(2)}) copy-start(bf16[256,1024]{1,0:T(8,128)(2,1)S(1)} %collective-permute-done.16.refs_2_) | copy-start | bytes 1572868
  279.5 18.2 %collective-permute-start.18 = (bf16[128,1024]{1,0:T(8,128)(2,1)S(1)}, bf16[128,1024]{1,0:T(8,128)(2,1)S(1)}, u32[]{:S(2)}, u32[]{:S(2)}) collective-permute-start(bf16[128,1024]{1,0:T(8,128)(2,1)S(1)} %slice.61), channel_id=1, source_target_pairs={{0,3},{1,0},{2,1},{3,2},{4,7},{5,4},{6,5},{7,6},{8,11},{9,8},{10,9... | collective-permute-start | bytes 786440 | tf_op jit(solution)/shard_map/ppermute | solution.py:481
  282.8 21.8 %copy-start.10 = (bf16[256,1024]{1,0:T(8,128)(2,1)}, bf16[256,1024]{1,0:T(8,128)(2,1)S(1)}, u32[]{:S(2)}) copy-start(bf16[256,1024]{1,0:T(8,128)(2,1)S(1)} %collective-permute-done.15.refs_1_) | copy-start | bytes 1572868
  282.9 18.5 %collective-permute-start.17 = (bf16[128,1024]{1,0:T(8,128)(2,1)S(1)}, bf16[128,1024]{1,0:T(8,128)(2,1)S(1)}, u32[]{:S(2)}, u32[]{:S(2)}) collective-permute-start(bf16[128,1024]{1,0:T(8,128)(2,1)S(1)} %slice.60), channel_id=1, source_target_pairs={{0,1},{1,2},{2,3},{3,0},{4,5},{5,6},{6,7},{7,4},{8,9},{9,10},{10,1... | collective-permute-start | bytes 786440 | tf_op jit(solution)/shard_map/ppermute | solution.py:481
  292.2 12.4 %copy-start.11 = (bf16[256,1024]{1,0:T(8,128)(2,1)}, bf16[256,1024]{1,0:T(8,128)(2,1)S(1)}, u32[]{:S(2)}) copy-start(bf16[256,1024]{1,0:T(8,128)(2,1)S(1)} %collective-permute-done.23.refs_7_) | copy-start | bytes 1572868
  292.2 9.2 %collective-permute-start.25 = (bf16[128,1024]{1,0:T(8,128)(2,1)S(1)}, bf16[128,1024]{1,0:T(8,128)(2,1)S(1)}, u32[]{:S(2)}, u32[]{:S(2)}) collective-permute-start(bf16[128,1024]{1,0:T(8,128)(2,1)S(1)} %slice.67), channel_id=1, source_target_pairs={{0,3},{1,0},{2,1},{3,2},{4,7},{5,4},{6,5},{7,6},{8,11},{9,8},{10,9... | collective-permute-start | bytes 786440 | tf_op jit(solution)/shard_map/ppermute | solution.py:481
  295.9 8.8 %copy-start.12 = (bf16[256,1024]{1,0:T(8,128)(2,1)}, bf16[256,1024]{1,0:T(8,128)(2,1)S(1)}, u32[]{:S(2)}) copy-start(bf16[256,1024]{1,0:T(8,128)(2,1)S(1)} %collective-permute-done.22.refs_6_) | copy-start | bytes 1572868
  295.9 8.7 %collective-permute-start.24 = (bf16[128,1024]{1,0:T(8,128)(2,1)S(1)}, bf16[128,1024]{1,0:T(8,128)(2,1)S(1)}, u32[]{:S(2)}, u32[]{:S(2)}) collective-permute-start(bf16[128,1024]{1,0:T(8,128)(2,1)S(1)} %slice.66), channel_id=1, source_target_pairs={{0,1},{1,2},{2,3},{3,0},{4,5},{5,6},{6,7},{7,4},{8,9},{9,10},{10,1... | collective-permute-start | bytes 786440 | tf_op jit(solution)/shard_map/ppermute | solution.py:481
  297.7 6.9 %copy-start.13 = (bf16[128,1024]{1,0:T(8,128)(2,1)}, bf16[128,1024]{1,0:T(8,128)(2,1)S(1)}, u32[]{:S(2)}) copy-start(bf16[128,1024]{1,0:T(8,128)(2,1)S(1)} %collective-permute-done.18.refs_4_) | copy-start | bytes 786436
  301.4 3.3 copy-start.14
  301.4 3.3 copy-start.15
  304.7 0.7 copy-start.16
